TPU v7x, 128 devices: a whole 4x4x4 slice. The times are simulated.
128 devices in a mesh: gx: 8 (over y, core), gy: 16 (over x, z).
Axes of the slice: x: 4, y: 4, z: 4, core: 2. Of those that a mesh axis runs over, the one named last changes fastest.
Arguments:
- near_tiles: bfloat16 [8, 16, 32, 20, 128, 128], P('gx', 'gy'), may hold values from -0.125 to 0.125
- block: bfloat16 [8, 16, 4096, 64], P('gx', 'gy'), may hold values from -7 to 7, as said below
- adjacency: int32 [8, 16, 32, 20], P('gx', 'gy'), may hold values from 0 to 4095, as said below
Outputs:
- basis: float32 [8, 16, 4096, 64], P('gx', 'gy')
- r_factor: float32 [64, 64], replicated
Inputs may be any that keep to these rules, and one draw needn't show every extreme that they name: `adjacency`: entry 0 of each row tile is the row tile itself; every entry names a tile of the device of its row tile or of a device whose gx and gy indices each differ by at most one, without wrapping. `block`: entries are real values of order one, within -7 to 7.
All inputs are finite; a program needn't handle non-finite values.
Results may differ from a plain program's by a relative error of at most 0.0003.
Values may be sent and summed in bfloat16 or wider, within the bound.
A program may use at most 128 MiB of HBM per device.

v0:
```python
import jax
import jax.numpy as jnp
from jax import lax
from jax.sharding import PartitionSpec as P


def extended(shard, sides, width):
    for axis, dim in sides:
        size, length = (lax.axis_size(axis), shard.shape[dim])
        up = [(i, (i + 1) % size) for i in range(size - 1)]
        down = [(j, i) for i, j in up]
        last = lax.slice_in_dim(shard, length - width, length, axis=dim)
        initial = lax.slice_in_dim(shard, 0, width, axis=dim)
        before = lax.ppermute(last, axis, up)
        after = lax.ppermute(initial, axis, down)
        shard = jnp.concatenate([before, shard, after], axis=dim)
    return shard


def swapped(value, axis, stride):
    mask = 2**stride
    pairs = [(source, source ^ mask) for source in range(lax.axis_size(axis))]
    return lax.ppermute(value, axis, pairs)


def upper_cholesky(matrix):
    return jnp.linalg.cholesky(matrix).T


def gram_of(matrix):
    return jnp.dot(matrix.T, matrix, precision=lax.Precision.HIGHEST)


def right_solve(values, factor):
    return jax.scipy.linalg.solve_triangular(factor.T, values.T, lower=True).T


def shards(near_tiles, block, adjacency):
    tiles_dev = adjacency.shape[2]
    tile_rows = near_tiles.shape[4]
    columns = block.shape[3]
    gy_count = lax.axis_size("gy")
    neighbours = extended(block, (("gx", 0), ("gy", 1)), 1)
    flat_rows = neighbours.reshape(9 * tiles_dev, tile_rows, columns)
    links = adjacency[0, 0]
    owner = links // tiles_dev
    offset_x = owner // gy_count - lax.axis_index("gx") + 1
    offset_y = owner % gy_count - lax.axis_index("gy") + 1
    local_tile = (offset_x * 3 + offset_y) * tiles_dev + links % tiles_dev
    picked = flat_rows[local_tile]
    product = jnp.einsum(
        "rnij,rnjk->rik", near_tiles[0, 0], picked, preferred_element_type=jnp.float32
    )
    image = product.reshape(tiles_dev * tile_rows, columns)
    scale = jnp.sqrt(jnp.float32(image.shape[0] * lax.axis_size("gx") * gy_count))
    factor = upper_cholesky(gram_of(image))
    for level in range(gy_count.bit_length() - 1):
        partner = swapped(factor, "gy", level)
        factor = upper_cholesky(gram_of(factor) + gram_of(partner))
    for level in range(lax.axis_size("gx").bit_length() - 1):
        partner = swapped(factor, "gx", level)
        factor = upper_cholesky(gram_of(factor) + gram_of(partner))
    ortho = right_solve(image, factor)
    basis = (ortho * scale).reshape(1, 1, image.shape[0], columns)
    return (basis, factor / scale)


def solution(mesh):
    in_specs = (
        P("gx", "gy", None, None, None, None),
        P("gx", "gy", None, None),
        P("gx", "gy", None, None),
    )
    out_specs = (P("gx", "gy", None, None), P())
    return jax.shard_map(shards, mesh=mesh, in_specs=in_specs, out_specs=out_specs, check_vma=False)
```

profile of v0, /device:TPU:1, one launch (start us, length us, event | category | flops | bytes accessed | tf_op | source)
XLA Modules:
  0.0 221.0 jit_solution(13803224493000363208)
XLA Ops:
  0.6 4.6 %collective-permute-start = (bf16[1,1,4096,64]{2,3,1,0:T(8,128)(2,1)}, bf16[1,1,4096,64]{2,3,1,0:T(8,128)(2,1)S(1)}, u32[]{:S(2)}, u32[]{:S(2)}) collective-permute-start(bf16[1,1,4096,64]{2,3,1,0:T(8,128)(2,1)} %param.5), channel_id=1, source_target_pairs={{0,16},{16,32},{32,48},{48,64},{64,80},{80,96},{96,112},{1,17},{17... | collective-permute-start | bytes 1572872 | tf_op jit(solution)/shard_map/ppermute | solution.py:14
  5.2 1.9 collective-permute-start.1
  7.2 4.5 %collective-permute-done = bf16[1,1,4096,64]{2,3,1,0:T(8,128)(2,1)S(1)} collective-permute-done((bf16[1,1,4096,64]{2,3,1,0:T(8,128)(2,1)}, bf16[1,1,4096,64]{2,3,1,0:T(8,128)(2,1)S(1)}, u32[]{:S(2)}, u32[]{:S(2)}) %collective-permute-start) | collective-permute-done | bytes 524320 | tf_op jit(solution)/shard_map/ppermute | solution.py:14
  11.7 1.1 constant_dynamic-update-slice_fusion.1
  12.8 3.5 %collective-permute-done.1 = bf16[1,1,4096,64]{2,3,1,0:T(8,128)(2,1)S(1)} collective-permute-done((bf16[1,1,4096,64]{2,3,1,0:T(8,128)(2,1)}, bf16[1,1,4096,64]{2,3,1,0:T(8,128)(2,1)S(1)}, u32[]{:S(2)}, u32[]{:S(2)}) %collective-permute-start.1) | collective-permute-done | bytes 524320 | tf_op jit(solution)/shard_map/ppermute | solution.py:15
  16.3 1.3 collective-permute-start.3
  17.6 5.3 %collective-permute-start.2 = (bf16[3,1,4096,64]{2,3,1,0:T(8,128)(2,1)S(1)}, bf16[3,1,4096,64]{2,3,1,0:T(8,128)(2,1)}, u32[]{:S(2)}, u32[]{:S(2)}) collective-permute-start(bf16[3,1,4096,64]{2,3,1,0:T(8,128)(2,1)S(1)} %constant_dynamic-update-slice_fusion), channel_id=1, source_target_pairs={{0,1},{1,2},{2,3},{3,4},{4,5},{5,6},{6,7},{7,8},{8,9},{9,10},{10,1... | collective-permute-start | bytes 4718600 | tf_op jit(solution)/shard_map/ppermute | solution.py:14
  24.0 23.8 %collective-permute-done.3 = bf16[3,1,4096,64]{2,3,1,0:T(8,128)(2,1)S(1)} collective-permute-done((bf16[3,1,4096,64]{2,3,1,0:T(8,128)(2,1)S(1)}, bf16[3,1,4096,64]{2,3,1,0:T(8,128)(2,1)S(1)}, u32[]{:S(2)}, u32[]{:S(2)}) %collective-permute-start.3) | collective-permute-done | bytes 1572896 | tf_op jit(solution)/shard_map/ppermute | solution.py:15
  47.8 1.8 collective-permute-done.2
  49.5 1.7 pad_maximum_fusion
  51.2 6.7 %copy.28 = bf16[3,3,4096,64]{2,1,0,3:T(4,128)(2,1)} copy(bf16[3,3,4096,64]{2,3,1,0:T(8,128)(2,1)S(1)} %pad_maximum_fusion) | data formatting | bytes 9437184 | tf_op jit(solution)/shard_map/concatenate | solution.py:16
  58.0 13.5 %reshape.214 = bf16[288,128,64]{1,0,2:T(8,128)(2,1)} reshape(bf16[3,3,4096,64]{2,1,0,3:T(4,128)(2,1)} %copy.28) | data formatting | bytes 9437184 | tf_op jit(solution)/shard_map/reshape | solution.py:44
  71.5 6.4 %copy.30 = bf16[288,128,64]{1,2,0:T(8,128)(2,1)} copy(bf16[288,128,64]{1,0,2:T(8,128)(2,1)} %reshape.214) | data formatting | bytes 9437184 | tf_op jit(solution)/shard_map/reshape | solution.py:44
  77.9 22.2 %gather_fusion = bf16[640,128,64]{1,2,0:T(8,128)(2,1)} fusion(bf16[288,128,64]{1,2,0:T(8,128)(2,1)} %copy.30, s32[1024]{0:T(1024)S(1)} %pad_clamp_fusion), kind=kCustom, calls=%fused_computation | custom fusion | bytes 20974080 | tf_op jit(solution)/shard_map/gather | solution.py:50
  100.0 13.7 %fusion = f32[32,64,128,1]{2,1,3,0:T(8,128)S(1)} fusion(bf16[32,20,128,64]{2,3,1,0:T(8,128)(2,1)} %bitcast.108, bf16[1,1,32,20,128,128]{5,4,3,2,1,0:T(8,128)(2,1)} %param.4), kind=kOutput, calls=%fused_computation.1 | convolution fusion | flops 1342177280 | bytes 32505856 | tf_op jit(solution)/shard_map/rnij,rnjk->rik/dot_general | solution.py:51
  113.7 1.0 convolution_bitcast_fusion
  114.8 5.8 %cholesky.134 = f32[64,64]{1,0:T(8,128)S(1)} custom-call(f32[64,64]{1,0:T(8,128)S(1)} %fusion.14), custom_call_target="Cholesky" | custom-call | tf_op jit(solution)/shard_map/jit(cholesky)/cholesky | solution.py:27
  122.0 2.1 collective-permute-start.4
  125.7 5.8 %cholesky.145 = f32[64,64]{1,0:T(8,128)S(1)} custom-call(f32[64,64]{1,0:T(8,128)S(1)} %fusion.13), custom_call_target="Cholesky" | custom-call | tf_op jit(solution)/shard_map/jit(cholesky)/cholesky | solution.py:27
  132.9 5.3 %collective-permute-start.5 = (f32[64,64]{0,1:T(8,128)S(1)}, f32[64,64]{0,1:T(8,128)S(1)}, u32[]{:S(2)}, u32[]{:S(2)}) collective-permute-start(f32[64,64]{0,1:T(8,128)S(1)} %fusion.31), channel_id=1, source_target_pairs={{0,2},{1,3},{2,0},{3,1},{4,6},{5,7},{6,4},{7,5},{8,10},{9,11},{10,... | collective-permute-start | bytes 49160 | tf_op jit(solution)/shard_map/ppermute | solution.py:23
  139.8 5.8 %cholesky.156 = f32[64,64]{1,0:T(8,128)S(1)} custom-call(f32[64,64]{1,0:T(8,128)S(1)} %fusion.12), custom_call_target="Cholesky" | custom-call | tf_op jit(solution)/shard_map/jit(cholesky)/cholesky | solution.py:27
  147.0 5.1 %collective-permute-start.6 = (f32[64,64]{0,1:T(8,128)S(1)}, f32[64,64]{0,1:T(8,128)S(1)}, u32[]{:S(2)}, u32[]{:S(2)}) collective-permute-start(f32[64,64]{0,1:T(8,128)S(1)} %fusion.33), channel_id=1, source_target_pairs={{0,4},{1,5},{2,6},{3,7},{4,0},{5,1},{6,2},{7,3},{8,12},{9,13},{10,... | collective-permute-start | bytes 49160 | tf_op jit(solution)/shard_map/ppermute | solution.py:23
  153.6 5.8 %cholesky.167 = f32[64,64]{1,0:T(8,128)S(1)} custom-call(f32[64,64]{1,0:T(8,128)S(1)} %fusion.11), custom_call_target="Cholesky" | custom-call | tf_op jit(solution)/shard_map/jit(cholesky)/cholesky | solution.py:27
  160.8 3.1 %collective-permute-start.7 = (f32[64,64]{0,1:T(8,128)S(1)}, f32[64,64]{0,1:T(8,128)S(1)}, u32[]{:S(2)}, u32[]{:S(2)}) collective-permute-start(f32[64,64]{0,1:T(8,128)S(1)} %fusion.35), channel_id=1, source_target_pairs={{0,8},{1,9},{2,10},{3,11},{4,12},{5,13},{6,14},{7,15},{8,0},{9,1},... | collective-permute-start | bytes 49160 | tf_op jit(solution)/shard_map/ppermute | solution.py:23
  165.5 5.8 %cholesky.178 = f32[64,64]{1,0:T(8,128)S(1)} custom-call(f32[64,64]{1,0:T(8,128)S(1)} %fusion.10), custom_call_target="Cholesky" | custom-call | tf_op jit(solution)/shard_map/jit(cholesky)/cholesky | solution.py:27
  174.2 5.8 %cholesky.189 = f32[64,64]{1,0:T(8,128)S(1)} custom-call(f32[64,64]{1,0:T(8,128)S(1)} %fusion.9), custom_call_target="Cholesky" | custom-call | tf_op jit(solution)/shard_map/jit(cholesky)/cholesky | solution.py:27
  181.4 11.1 %collective-permute-start.9 = (f32[64,64]{0,1:T(8,128)S(1)}, f32[64,64]{0,1:T(8,128)S(1)}, u32[]{:S(2)}, u32[]{:S(2)}) collective-permute-start(f32[64,64]{0,1:T(8,128)S(1)} %fusion.39), channel_id=1, source_target_pairs={{0,32},{16,48},{32,0},{48,16},{64,96},{80,112},{96,64},{112,80},{1... | collective-permute-start | bytes 49160 | tf_op jit(solution)/shard_map/ppermute | solution.py:23
  194.1 5.8 %cholesky.200 = f32[64,64]{1,0:T(8,128)S(1)} custom-call(f32[64,64]{1,0:T(8,128)S(1)} %fusion.8), custom_call_target="Cholesky" | custom-call | tf_op jit(solution)/shard_map/jit(cholesky)/cholesky | solution.py:27
  201.2 3.4 %collective-permute-start.10 = (f32[64,64]{0,1:T(8,128)S(1)}, f32[64,64]{0,1:T(8,128)S(1)}, u32[]{:S(2)}, u32[]{:S(2)}) collective-permute-start(f32[64,64]{0,1:T(8,128)S(1)} %fusion.41), channel_id=1, source_target_pairs={{0,64},{16,80},{32,96},{48,112},{64,0},{80,16},{96,32},{112,48},{1... | collective-permute-start | bytes 49160 | tf_op jit(solution)/shard_map/ppermute | solution.py:23
  206.2 5.8 %cholesky.211 = f32[64,64]{1,0:T(8,128)S(1)} custom-call(f32[64,64]{1,0:T(8,128)S(1)} %fusion.7), custom_call_target="Cholesky" | custom-call | tf_op jit(solution)/shard_map/jit(cholesky)/cholesky | solution.py:27
  214.1 4.9 %custom-call.6 = f32[1,64,64]{1,2,0:T(8,128)S(1)} custom-call(f32[1,64,64]{2,1,0:T(8,128)S(1)} %get-tuple-element.8), custom_call_target="InvertDiagBlocksLowerTriangular" | custom-call | tf_op jit(solution)/shard_map/jit(_solve_triangular)/triangular_solve | solution.py:35
  219.0 2.0 fusion.2
  (69 shorter events, 23.5 us)
Async XLA Ops:
  0.6 11.0 %collective-permute-start = (bf16[1,1,4096,64]{2,3,1,0:T(8,128)(2,1)}, bf16[1,1,4096,64]{2,3,1,0:T(8,128)(2,1)S(1)}, u32[]{:S(2)}, u32[]{:S(2)}) collective-permute-start(bf16[1,1,4096,64]{2,3,1,0:T(8,128)(2,1)} %param.5), channel_id=1, source_target_pairs={{0,16},{16,32},{32,48},{48,64},{64,80},{80,96},{96,112},{1,17},{17... | collective-permute-start | bytes 1572872 | tf_op jit(solution)/shard_map/ppermute | solution.py:14
  5.2 11.0 %collective-permute-start.1 = (bf16[1,1,4096,64]{2,3,1,0:T(8,128)(2,1)}, bf16[1,1,4096,64]{2,3,1,0:T(8,128)(2,1)S(1)}, u32[]{:S(2)}, u32[]{:S(2)}) collective-permute-start(bf16[1,1,4096,64]{2,3,1,0:T(8,128)(2,1)} %param.5), channel_id=1, source_target_pairs={{16,0},{32,16},{48,32},{64,48},{80,64},{96,80},{112,96},{17,1},{33... | collective-permute-start | bytes 1572872 | tf_op jit(solution)/shard_map/ppermute | solution.py:15
  16.3 31.5 %collective-permute-start.3 = (bf16[3,1,4096,64]{2,3,1,0:T(8,128)(2,1)S(1)}, bf16[3,1,4096,64]{2,3,1,0:T(8,128)(2,1)S(1)}, u32[]{:S(2)}, u32[]{:S(2)}) collective-permute-start(bf16[3,1,4096,64]{2,3,1,0:T(8,128)(2,1)S(1)} %constant_dynamic-update-slice_fusion), channel_id=1, source_target_pairs={{1,0},{2,1},{3,2},{4,3},{5,4},{6,5},{7,6},{8,7},{9,8},{10,9},{11,1... | collective-permute-start | bytes 4718600 | tf_op jit(solution)/shard_map/ppermute | solution.py:15
  17.6 32.0 %collective-permute-start.2 = (bf16[3,1,4096,64]{2,3,1,0:T(8,128)(2,1)S(1)}, bf16[3,1,4096,64]{2,3,1,0:T(8,128)(2,1)}, u32[]{:S(2)}, u32[]{:S(2)}) collective-permute-start(bf16[3,1,4096,64]{2,3,1,0:T(8,128)(2,1)S(1)} %constant_dynamic-update-slice_fusion), channel_id=1, source_target_pairs={{0,1},{1,2},{2,3},{3,4},{4,5},{5,6},{6,7},{7,8},{8,9},{9,10},{10,1... | collective-permute-start | bytes 4718600 | tf_op jit(solution)/shard_map/ppermute | solution.py:14
  122.0 3.4 %collective-permute-start.4 = (f32[64,64]{0,1:T(8,128)S(1)}, f32[64,64]{0,1:T(8,128)S(1)}, u32[]{:S(2)}, u32[]{:S(2)}) collective-permute-start(f32[64,64]{0,1:T(8,128)S(1)} %fusion.29), channel_id=1, source_target_pairs={{0,1},{1,0},{2,3},{3,2},{4,5},{5,4},{6,7},{7,6},{8,9},{9,8},{10,11... | collective-permute-start | bytes 49160 | tf_op jit(solution)/shard_map/ppermute | solution.py:23
  132.9 6.6 %collective-permute-start.5 = (f32[64,64]{0,1:T(8,128)S(1)}, f32[64,64]{0,1:T(8,128)S(1)}, u32[]{:S(2)}, u32[]{:S(2)}) collective-permute-start(f32[64,64]{0,1:T(8,128)S(1)} %fusion.31), channel_id=1, source_target_pairs={{0,2},{1,3},{2,0},{3,1},{4,6},{5,7},{6,4},{7,5},{8,10},{9,11},{10,... | collective-permute-start | bytes 49160 | tf_op jit(solution)/shard_map/ppermute | solution.py:23
  147.0 6.4 %collective-permute-start.6 = (f32[64,64]{0,1:T(8,128)S(1)}, f32[64,64]{0,1:T(8,128)S(1)}, u32[]{:S(2)}, u32[]{:S(2)}) collective-permute-start(f32[64,64]{0,1:T(8,128)S(1)} %fusion.33), channel_id=1, source_target_pairs={{0,4},{1,5},{2,6},{3,7},{4,0},{5,1},{6,2},{7,3},{8,12},{9,13},{10,... | collective-permute-start | bytes 49160 | tf_op jit(solution)/shard_map/ppermute | solution.py:23
  160.8 4.4 %collective-permute-start.7 = (f32[64,64]{0,1:T(8,128)S(1)}, f32[64,64]{0,1:T(8,128)S(1)}, u32[]{:S(2)}, u32[]{:S(2)}) collective-permute-start(f32[64,64]{0,1:T(8,128)S(1)} %fusion.35), channel_id=1, source_target_pairs={{0,8},{1,9},{2,10},{3,11},{4,12},{5,13},{6,14},{7,15},{8,0},{9,1},... | collective-permute-start | bytes 49160 | tf_op jit(solution)/shard_map/ppermute | solution.py:23
  172.7 1.3 collective-permute-start.8
  181.4 12.4 %collective-permute-start.9 = (f32[64,64]{0,1:T(8,128)S(1)}, f32[64,64]{0,1:T(8,128)S(1)}, u32[]{:S(2)}, u32[]{:S(2)}) collective-permute-start(f32[64,64]{0,1:T(8,128)S(1)} %fusion.39), channel_id=1, source_target_pairs={{0,32},{16,48},{32,0},{48,16},{64,96},{80,112},{96,64},{112,80},{1... | collective-permute-start | bytes 49160 | tf_op jit(solution)/shard_map/ppermute | solution.py:23
  201.2 4.7 %collective-permute-start.10 = (f32[64,64]{0,1:T(8,128)S(1)}, f32[64,64]{0,1:T(8,128)S(1)}, u32[]{:S(2)}, u32[]{:S(2)}) collective-permute-start(f32[64,64]{0,1:T(8,128)S(1)} %fusion.41), channel_id=1, source_target_pairs={{0,64},{16,80},{32,96},{48,112},{64,0},{80,16},{96,32},{112,48},{1... | collective-permute-start | bytes 49160 | tf_op jit(solution)/shard_map/ppermute | solution.py:23
where the time goes:
time: 224 us; the launch traced here: 221 us
  other arithmetic  64.9 us (29%)
  local copies, waits for them, and re-layouts  51.4 us (23%)
  starting transfers between devices  43.2 us (19%)
  waiting for transfers between devices  36.7 us (16%)
  matrix products  23.8 us (11%)
    another operation x24, other arithmetic, upper_cholesky(): return jnp.linalg.cholesky(matrix).T  52.2 us
    ppermute x7, starting transfers between devices, swapped(): return lax.ppermute(value, axis, pairs)  30.1 us
    ppermute x2, waiting for transfers between devices, extended(): after = lax.ppermute(initial, axis, down)  27.2 us
    gather x1, local copies, waits for them, and re-layouts, shards(): picked = flat_rows[local_tile]  22.2 us
    reshape x2, local copies, waits for them, and re-layouts, shards(): flat_rows = neighbours.reshape(9 * tiles_dev, tile_rows, columns)  19.9 us
    dot_general x1, matrix products, shards(): jnp.einsum('rnij,rnjk->rik', near_tiles[0, 0], picked, preferred_element_...  13.7 us
    ppermute x2, starting transfers between devices, extended(): before = lax.ppermute(last, axis, up)  9.93 us
    dot_general x15, matrix products, gram_of(): return jnp.dot(matrix.T, matrix, precision=lax.Precision.HIGHEST)  8.06 us
  transfers between devices with their start and end apart: 11, of which 11 were waited for; matrix products, arithmetic and copies ran while one was open for 4% of the time, Pallas kernels for 0%

commit v1 on v0

v1 whole, which is shorter than its diff:
```python
import functools

import jax
import jax.numpy as jnp
from jax import lax
from jax.experimental import pallas as pl
from jax.experimental.pallas import tpu as pltpu
from jax.sharding import PartitionSpec as P

K = 64
TILE = 128
NB = 20
TILES = 32
ROWS_DEV = TILES * TILE
N_GX = 8
N_GY = 16
ROWS = ROWS_DEV * N_GX * N_GY
CHUNKS = 4
PART = TILES // CHUNKS
A_COPIES = 8
UNROLL = 8
MESH = pl.DeviceIdType.MESH


def slot_of(x, y):
    return (lax.rem(x, 4) * 4 + lax.rem(y, 4)) * TILES


def folded(gram):
    rows = gram[:K] + gram[K:]
    both = rows + pltpu.roll(rows, K, 1)
    lane = lax.broadcasted_iota(jnp.int32, (K // 2, 2 * K), 1)
    return jnp.where(lane < K, both[: K // 2], both[K // 2 :])


def product_kernel(
    tiles_hbm, block_hbm, places, split_ref, gram_ref,
    tiles, table, turned, across_x, across_y,
    tile_sem, own_sem, gy_send, gy_recv, gx_send, gx_recv, sx_send, sx_recv, sy_send, sy_recv,
):
    me_x, me_y = lax.axis_index("gx"), lax.axis_index("gy")

    def ring_x(step):
        return lax.rem(me_x + step + N_GX, N_GX)

    def ring_y(step):
        return lax.rem(me_y + step + N_GY, N_GY)

    own = slot_of(me_x, me_y)
    own_copy = pltpu.make_async_copy(block_hbm, turned, own_sem)
    own_copy.start()

    barrier = pltpu.get_barrier_semaphore()
    for step in range(1, N_GX):
        pl.semaphore_signal(barrier, inc=1, device_id=(ring_x(step), me_y), device_id_type=MESH)
    for step in range(1, N_GY):
        pl.semaphore_signal(barrier, inc=1, device_id=(me_x, ring_y(step)), device_id_type=MESH)
    own_copy.wait()
    for i in range(TILES):
        table[own + i] = turned[:, i * TILE : (i + 1) * TILE]
    pl.semaphore_wait(barrier, N_GX + N_GY - 2)

    started = []

    def span(slot, part):
        return table.at[pl.ds(slot + part * PART, PART)]

    def push(slot, part, send, recv, device):
        copy = pltpu.make_async_remote_copy(
            src_ref=span(slot, part), dst_ref=span(slot, part), send_sem=send, recv_sem=recv,
            device_id=device, device_id_type=MESH,
        )
        copy.start()
        started.append(copy)

    def push_x(slot, which, part):
        for d, step in enumerate((1, -1)):
            push(slot, part, gx_send.at[d, which, part], gx_recv.at[d, which, part], (ring_x(step), me_y))

    for part in range(CHUNKS):
        for d, step in enumerate((1, -1)):
            push(own, part, gy_send.at[d, part], gy_recv.at[d, part], (me_x, ring_y(step)))
        push_x(own, 0, part)

    copies = []
    group = TILES // A_COPIES
    for i in range(A_COPIES):
        copy = pltpu.make_async_copy(
            tiles_hbm.at[pl.ds(i * group, group)], tiles.at[pl.ds(i * group, group)], tile_sem.at[i]
        )
        copy.start()
        copies.append(copy)

    def landed(slot, part, sem):
        pltpu.make_async_copy(span(slot, part), span(slot, part), sem).wait()

    for part in range(CHUNKS):
        for d, step in enumerate((-1, 1)):
            slot = slot_of(me_x, ring_y(step))
            landed(slot, part, gy_recv.at[d, part])
            push_x(slot, 1 + d, part)
    for copy in copies:
        copy.wait()
    for which, dy in enumerate((0, -1, 1)):
        for part in range(CHUNKS):
            for d, step in enumerate((-1, 1)):
                landed(slot_of(ring_x(step), ring_y(dy)), part, gx_recv.at[d, which, part])

    def row_tile(t, carry):
        near = jnp.concatenate([tiles[t, j] for j in range(NB)], axis=1)
        rows = jnp.concatenate([table[places[j, t]] for j in range(NB)], axis=1)
        image = lax.dot_general(
            near, rows, (((1,), (1,)), ((), ())), preferred_element_type=jnp.float32
        ).T
        high = image.astype(jnp.bfloat16)
        low = (image - high.astype(jnp.float32)).astype(jnp.bfloat16)
        here = pl.ds(pl.multiple_of(t * TILE, TILE), TILE)
        split_ref[:K, here] = high
        split_ref[K:, here] = low
        return carry

    lax.fori_loop(0, TILES, row_tile, 0, unroll=UNROLL)
    split = split_ref[...]
    gram = lax.dot_general(split, split, (((1,), (1,)), ((), ())), preferred_element_type=jnp.float32)

    def summed(value, gathered, count, me, send, recv, device):
        gathered[me] = value
        sends = []
        for step in range(1, count):
            copy = pltpu.make_async_remote_copy(
                src_ref=gathered.at[me], dst_ref=gathered.at[me], send_sem=send.at[step], recv_sem=recv.at[step],
                device_id=device(step), device_id_type=MESH,
            )
            copy.start()
            sends.append(copy)
        for step in range(1, count):
            source = gathered.at[lax.rem(me - step + count, count)]
            pltpu.make_async_copy(source, source, recv.at[step]).wait()
        terms = [gathered[i] for i in range(count)]
        while len(terms) > 1:
            terms = [a + b for a, b in zip(terms[::2], terms[1::2])]
        return terms[0], sends

    partial, sends_x = summed(
        folded(gram), across_x, N_GX, me_x, sx_send, sx_recv, lambda step: (ring_x(step), me_y)
    )
    total, sends_y = summed(
        partial, across_y, N_GY, me_y, sy_send, sy_recv, lambda step: (me_x, ring_y(step))
    )
    swapped = pltpu.roll(total, K, 1)
    lane = lax.broadcasted_iota(jnp.int32, total.shape, 1)
    gram_ref[: K // 2] = jnp.where(lane < K, total, swapped)
    gram_ref[K // 2 :] = jnp.where(lane < K, swapped, total)
    for copy in started + sends_x + sends_y:
        copy.wait_send()


def eliminated(rows):
    count = K // 8
    sub = lax.broadcasted_iota(jnp.int32, (8, 128), 0)
    zero = jnp.zeros((8, 128), jnp.float32)

    def spread(x):
        return jnp.broadcast_to(x, (8, 128))

    pivots = []
    for p in range(count):
        columns = [
            {r: spread(rows[r][:, 8 * p + j : 8 * p + j + 1]) for r in range(p, count)} for j in range(8)
        ]
        found = zero
        for j in range(8):
            pivot = spread(columns[j][p][j : j + 1])
            found = jnp.where(sub == j, pivot, found)
            inverse = 1.0 / pivot
            pivot_row = spread(rows[p][j : j + 1])
            later = {i: spread(columns[i][p][j : j + 1]) for i in range(j + 1, 8)}
            for r in range(p, count):
                scaled = columns[j][r] * inverse
                if r == p:
                    scaled = jnp.where(sub > j, scaled, zero)
                for i in range(j + 1, 8):
                    columns[i][r] = columns[i][r] - scaled * later[i]
                rows[r] = rows[r] - scaled * pivot_row
        pivots.append(found)
    return rows, pivots


BASIS_PARTS = 4


def basis_kernel(gram_ref, split_hbm, basis_hbm, factor_ref, split, basis, sems):
    fetch = pltpu.make_async_copy(split_hbm, split, sems.at[BASIS_PARTS])
    fetch.start()
    lane = lax.broadcasted_iota(jnp.int32, (8, 128), 1)
    sub = lax.broadcasted_iota(jnp.int32, (8, 128), 0)
    count = K // 8
    rows = [
        jnp.where(lane < K, gram_ref[8 * r : 8 * r + 8], jnp.where(lane - K == sub + 8 * r, 1.0, 0.0))
        for r in range(count)
    ]
    rows, pivots = eliminated(rows)
    scale = float(ROWS) ** 0.5
    highs, lows = [], []
    for r in range(count):
        root = lax.rsqrt(pivots[r])
        root = root * (1.5 - 0.5 * pivots[r] * root * root)
        upper = rows[r] * root
        factor_ref[8 * r : 8 * r + 8] = (jnp.where(lane >= sub + 8 * r, upper, 0.0) * (1.0 / scale))[:, :K]
        solve = upper * scale
        solve = jnp.where(lane < K, pltpu.roll(solve, K, 1), solve)
        high = solve.astype(jnp.bfloat16)
        highs.append(high)
        lows.append((solve - high.astype(jnp.float32)).astype(jnp.bfloat16))
    solver = jnp.concatenate([jnp.concatenate(highs, 0), jnp.concatenate(lows, 0)], 1)
    fetch.wait()
    width = ROWS_DEV // BASIS_PARTS
    stores = []
    for part in range(BASIS_PARTS):
        here = slice(part * width, (part + 1) * width)
        image = split[:, here]
        basis[:, here] = jnp.dot(solver, jnp.concatenate([image, image], 0), preferred_element_type=jnp.float32)
        at = pl.ds(part * width, width)
        store = pltpu.make_async_copy(basis.at[:, at], basis_hbm.at[:, at], sems.at[part])
        store.start()
        stores.append(store)
    for store in stores:
        store.wait()


def shards(near_tiles, block, adjacency):
    any_space, vmem, smem = (
        pl.BlockSpec(memory_space=space) for space in (pl.ANY, pltpu.VMEM, pltpu.SMEM)
    )
    dma = pltpu.SemaphoreType.DMA
    links = jnp.swapaxes(adjacency[0, 0], 0, 1)
    owner = links // TILES
    places = slot_of(owner // N_GY, owner % N_GY) + links % TILES
    split, gram = pl.pallas_call(
        product_kernel,
        name="near_product",
        out_shape=(
            jax.ShapeDtypeStruct((2 * K, ROWS_DEV), jnp.bfloat16),
            jax.ShapeDtypeStruct((K, 2 * K), jnp.float32),
        ),
        in_specs=[any_space, any_space, smem],
        out_specs=(vmem, vmem),
        scratch_shapes=[
            pltpu.VMEM((TILES, NB, TILE, TILE), jnp.bfloat16),
            pltpu.VMEM((16 * TILES, K, TILE), jnp.bfloat16),
            pltpu.VMEM((K, ROWS_DEV), jnp.bfloat16),
            pltpu.VMEM((N_GX, K // 2, 2 * K), jnp.float32),
            pltpu.VMEM((N_GY, K // 2, 2 * K), jnp.float32),
            dma((A_COPIES,)),
            dma,
            dma((2, CHUNKS)),
            dma((2, CHUNKS)),
            dma((2, 3, CHUNKS)),
            dma((2, 3, CHUNKS)),
            dma((N_GX,)),
            dma((N_GX,)),
            dma((N_GY,)),
            dma((N_GY,)),
        ],
        compiler_params=pltpu.CompilerParams(
            collective_id=0, has_side_effects=True, vmem_limit_bytes=56 * 1024 * 1024
        ),
    )(near_tiles[0, 0], jnp.swapaxes(block[0, 0], 0, 1), places)
    basis, factor = pl.pallas_call(
        basis_kernel,
        name="orthonormal_basis",
        out_shape=(
            jax.ShapeDtypeStruct((K, ROWS_DEV), jnp.float32),
            jax.ShapeDtypeStruct((K, K), jnp.float32),
        ),
        in_specs=[vmem, any_space],
        out_specs=(any_space, vmem),
        scratch_shapes=[
            pltpu.VMEM((2 * K, ROWS_DEV), jnp.bfloat16),
            pltpu.VMEM((K, ROWS_DEV), jnp.float32),
            dma((BASIS_PARTS + 1,)),
        ],
    )(gram, split)
    return (jnp.swapaxes(basis, 0, 1).reshape(1, 1, ROWS_DEV, K), factor)


def solution(mesh):
    in_specs = (
        P("gx", "gy", None, None, None, None),
        P("gx", "gy", None, None),
        P("gx", "gy", None, None),
    )
    out_specs = (P("gx", "gy", None, None), P())
    return jax.shard_map(shards, mesh=mesh, in_specs=in_specs, out_specs=out_specs, check_vma=False)
```

time: 224 us -> 54 us (0.24); the launches traced: 221 us -> 53.6 us
  other arithmetic: 64.9 us -> 1.34 us
  Pallas kernels: 0 us -> 51.6 us
  local copies, waits for them, and re-layouts: 51.4 us -> 0 us
  starting transfers between devices: 43.2 us -> 0 us
  waiting for transfers between devices: 36.7 us -> 0 us
  matrix products: 23.8 us -> 0 us
    another operation x25 -> x0, other arithmetic: 57.1 us -> none  [the longest x24 52.2 us: upper_cholesky(): return jnp.linalg.cholesky(matrix).T]
    pallas_call x0 -> x2, Pallas kernels: none -> 51.6 us  [the longest x1 46.3 us: shards(): pl.pallas_call(product_kernel, name='near_product', out_shape=(jax.ShapeD...]
    ppermute x11 -> x0, starting transfers between devices: 43.2 us -> none  [the longest x7 30.1 us: swapped(): return lax.ppermute(value, axis, pairs)]
    ppermute x11 -> x0, waiting for transfers between devices: 36.7 us -> none  [the longest x2 27.2 us: extended(): after = lax.ppermute(initial, axis, down)]
    gather x1 -> x0, local copies, waits for them, and re-layouts: 22.2 us -> none  [shards(): picked = flat_rows[local_tile]]
    dot_general x16 -> x0, matrix products: 21.8 us -> none  [the longest x1 13.7 us: shards(): jnp.einsum('rnij,rnjk->rik', near_tiles[0, 0], picked, preferred_element_...]
    reshape x2 -> x0, local copies, waits for them, and re-layouts: 19.9 us -> none  [shards(): flat_rows = neighbours.reshape(9 * tiles_dev, tile_rows, columns)]
    concatenate x2 -> x0, local copies, waits for them, and re-layouts: 6.76 us -> none  [extended(): shard = jnp.concatenate([before, shard, after], axis=dim)]
  transfers between devices with their start and end apart: 11 -> 0, of which waited for: 11 -> 0; matrix products, arithmetic and copies ran while one was open for 4% -> 0% of each run, Pallas kernels for 0% -> 0%
where the time goes in v1:
time: 54 us; the launch traced here: 53.6 us
  Pallas kernels  51.6 us (96%)
  other arithmetic  1.34 us (2%)
  between operations  0.64 us (1%)
    pallas_call x1, Pallas kernels, shards(): pl.pallas_call(product_kernel, name='near_product', out_shape=(jax.ShapeD...  46.3 us
    pallas_call x1, Pallas kernels, shards(): pl.pallas_call(basis_kernel, name='orthonormal_basis', out_shape=(jax.Sha...  5.27 us
    add x1, other arithmetic, shards(): places = slot_of(owner // N_GY, owner % N_GY) + links % TILES  1.34 us

profile of v1, /device:TPU:1, one launch (start us, length us, event | category | flops | bytes accessed | tf_op | source)
XLA Modules:
  0.0 53.6 jit_solution(10033780607319840190)
XLA Ops:
  0.6 1.3 %fusion.4.places = s32[20,32]{1,0:T(8,128)} fusion(s32[1,1,32,20]{2,1,3,0:T(1,128)} %param.5), kind=kLoop, calls=%fused_computation.18 | loop fusion | flops 34560 | bytes 5120 | tf_op jit(solution)/shard_map/add | solution.py:238
  2.0 46.3 %near_product.1 = (bf16[128,4096]{1,0:T(8,128)(2,1)}, f32[64,128]{1,0:T(8,128)}) custom-call(bf16[32,20,128,128]{3,2,1,0:T(8,128)(2,1)} %bitcast.25, bf16[64,4096]{1,0:T(8,128)(2,1)} %bitcast.26, s32[20,32]{1,0:T(8,128)} %fusion.4.places), custom_call_target="tpu_custom_call" | custom-call | tf_op jit(solution)/shard_map/near_product/pallas_call | solution.py:239
  48.3 5.3 %orthonormal_basis.1 = (f32[64,4096]{1,0:T(8,128)}, f32[64,64]{1,0:T(8,128)}) custom-call(f32[64,128]{1,0:T(8,128)} %get-tuple-element.6.gram_ref, bf16[128,4096]{1,0:T(8,128)(2,1)} %get-tuple-element.7.split_hbm), custom_call_target="tpu_custom_call" | custom-call | tf_op jit(solution)/shard_map/orthonormal_basis/pallas_call | solution.py:269

commit v2 on v1

--- a/solution.py
+++ b/solution.py
@@ -16,6 +16,8 @@
 N_GY = 16
 ROWS = ROWS_DEV * N_GX * N_GY
 CHUNKS = 4
+TURNED = 1
+TURN_AT = 2
 PART = TILES // CHUNKS
 A_COPIES = 8
 UNROLL = 8
@@ -34,9 +36,10 @@
 
 
 def product_kernel(
-    tiles_hbm, block_hbm, places, split_ref, gram_ref,
-    tiles, table, turned, across_x, across_y,
-    tile_sem, own_sem, gy_send, gy_recv, gx_send, gx_recv, sx_send, sx_recv, sy_send, sy_recv,
+    tiles_hbm, block_hbm, links_hbm, split, gram_ref,
+    tiles, table, turned, links, across_x, across_y,
+    tile_sem, own_sem, gy_send, gy_recv, near_send, near_recv, far_send, far_recv, turn_send, turn_recv,
+    sx_send, sx_recv, sy_send, sy_recv, links_sem,
 ):
     me_x, me_y = lax.axis_index("gx"), lax.axis_index("gy")
 
@@ -46,15 +49,24 @@
     def ring_y(step):
         return lax.rem(me_y + step + N_GY, N_GY)
 
+    core = lax.rem(me_x, 2)
+    near_x = me_x + 1 - 2 * core
+    far_x = ring_x(2 * core - 1)
     own = slot_of(me_x, me_y)
+
+    barrier = pltpu.get_barrier_semaphore()
+
+    def greet(x, y):
+        pl.semaphore_signal(barrier, inc=1, device_id=(x, y), device_id_type=MESH)
+
+    for step in sorted(range(1, N_GY), key=lambda n: min(n, N_GY - n)):
+        greet(me_x, ring_y(step))
+    for step in sorted(range(1, N_GX), key=lambda n: min(n, N_GX - n)):
+        greet(ring_x(step), me_y)
     own_copy = pltpu.make_async_copy(block_hbm, turned, own_sem)
     own_copy.start()
-
-    barrier = pltpu.get_barrier_semaphore()
-    for step in range(1, N_GX):
-        pl.semaphore_signal(barrier, inc=1, device_id=(ring_x(step), me_y), device_id_type=MESH)
-    for step in range(1, N_GY):
-        pl.semaphore_signal(barrier, inc=1, device_id=(me_x, ring_y(step)), device_id_type=MESH)
+    links_copy = pltpu.make_async_copy(links_hbm, links, links_sem)
+    links_copy.start()
     own_copy.wait()
     for i in range(TILES):
         table[own + i] = turned[:, i * TILE : (i + 1) * TILE]
@@ -65,22 +77,22 @@
     def span(slot, part):
         return table.at[pl.ds(slot + part * PART, PART)]
 
-    def push(slot, part, send, recv, device):
+    def push(slot, part, send, recv, x, y):
         copy = pltpu.make_async_remote_copy(
             src_ref=span(slot, part), dst_ref=span(slot, part), send_sem=send, recv_sem=recv,
-            device_id=device, device_id_type=MESH,
+            device_id=(x, y), device_id_type=MESH,
         )
         copy.start()
         started.append(copy)
 
-    def push_x(slot, which, part):
-        for d, step in enumerate((1, -1)):
-            push(slot, part, gx_send.at[d, which, part], gx_recv.at[d, which, part], (ring_x(step), me_y))
+    def landed(slot, part, sem):
+        pltpu.make_async_copy(span(slot, part), span(slot, part), sem).wait()
 
     for part in range(CHUNKS):
         for d, step in enumerate((1, -1)):
-            push(own, part, gy_send.at[d, part], gy_recv.at[d, part], (me_x, ring_y(step)))
-        push_x(own, 0, part)
+            push(own, part, gy_send.at[d, part], gy_recv.at[d, part], me_x, ring_y(step))
+        push(own, part, far_send.at[0, part], far_recv.at[0, part], far_x, me_y)
+        push(own, part, near_send.at[0, part], near_recv.at[0, part], near_x, me_y)
 
     copies = []
     group = TILES // A_COPIES
@@ -91,37 +103,51 @@
         copy.start()
         copies.append(copy)
 
-    def landed(slot, part, sem):
-        pltpu.make_async_copy(span(slot, part), span(slot, part), sem).wait()
-
+    early = CHUNKS - TURNED
     for part in range(CHUNKS):
         for d, step in enumerate((-1, 1)):
             slot = slot_of(me_x, ring_y(step))
             landed(slot, part, gy_recv.at[d, part])
-            push_x(slot, 1 + d, part)
+            if part < early:
+                push(slot, part, far_send.at[1 + d, part], far_recv.at[1 + d, part], far_x, me_y)
+            push(slot, part, near_send.at[1 + d, part], near_recv.at[1 + d, part], near_x, me_y)
+        if part == TURN_AT:
+            for late in range(TURNED):
+                slot = slot_of(far_x, me_y)
+                landed(slot, early + late, far_recv.at[0, early + late])
+                for d, step in enumerate((1, -1)):
+                    push(slot, early + late, turn_send.at[d, late], turn_recv.at[d, late], me_x, ring_y(step))
+    links_copy.wait()
     for copy in copies:
         copy.wait()
     for which, dy in enumerate((0, -1, 1)):
         for part in range(CHUNKS):
-            for d, step in enumerate((-1, 1)):
-                landed(slot_of(ring_x(step), ring_y(dy)), part, gx_recv.at[d, which, part])
+            landed(slot_of(near_x, ring_y(dy)), part, near_recv.at[which, part])
+            if part < early:
+                landed(slot_of(far_x, ring_y(dy)), part, far_recv.at[which, part])
+            elif which:
+                landed(slot_of(far_x, ring_y(dy)), part, turn_recv.at[which - 1, part - early])
 
     def row_tile(t, carry):
         near = jnp.concatenate([tiles[t, j] for j in range(NB)], axis=1)
-        rows = jnp.concatenate([table[places[j, t]] for j in range(NB)], axis=1)
+        picked = []
+        for j in range(NB):
+            link = links[j, 0, t]
+            picked.append(table[((link >> 2) & (12 * TILES)) | (link & (4 * TILES - 1))])
+        rows = jnp.concatenate(picked, axis=1)
         image = lax.dot_general(
             near, rows, (((1,), (1,)), ((), ())), preferred_element_type=jnp.float32
         ).T
         high = image.astype(jnp.bfloat16)
         low = (image - high.astype(jnp.float32)).astype(jnp.bfloat16)
         here = pl.ds(pl.multiple_of(t * TILE, TILE), TILE)
-        split_ref[:K, here] = high
-        split_ref[K:, here] = low
+        split[:K, here] = high
+        split[K:, here] = low
         return carry
 
     lax.fori_loop(0, TILES, row_tile, 0, unroll=UNROLL)
-    split = split_ref[...]
-    gram = lax.dot_general(split, split, (((1,), (1,)), ((), ())), preferred_element_type=jnp.float32)
+    image = split[...]
+    gram = lax.dot_general(image, image, (((1,), (1,)), ((), ())), preferred_element_type=jnp.float32)
 
     def summed(value, gathered, count, me, send, recv, device):
         gathered[me] = value
@@ -189,9 +215,7 @@
 BASIS_PARTS = 4
 
 
-def basis_kernel(gram_ref, split_hbm, basis_hbm, factor_ref, split, basis, sems):
-    fetch = pltpu.make_async_copy(split_hbm, split, sems.at[BASIS_PARTS])
-    fetch.start()
+def basis_kernel(gram_ref, split, basis_hbm, factor_ref, basis, sems):
     lane = lax.broadcasted_iota(jnp.int32, (8, 128), 1)
     sub = lax.broadcasted_iota(jnp.int32, (8, 128), 0)
     count = K // 8
@@ -213,7 +237,6 @@
         highs.append(high)
         lows.append((solve - high.astype(jnp.float32)).astype(jnp.bfloat16))
     solver = jnp.concatenate([jnp.concatenate(highs, 0), jnp.concatenate(lows, 0)], 1)
-    fetch.wait()
     width = ROWS_DEV // BASIS_PARTS
     stores = []
     for part in range(BASIS_PARTS):
@@ -229,13 +252,10 @@
 
 
 def shards(near_tiles, block, adjacency):
-    any_space, vmem, smem = (
-        pl.BlockSpec(memory_space=space) for space in (pl.ANY, pltpu.VMEM, pltpu.SMEM)
-    )
+    hbm, vmem = (pl.BlockSpec(memory_space=space) for space in (pltpu.HBM, pltpu.VMEM))
     dma = pltpu.SemaphoreType.DMA
-    links = jnp.swapaxes(adjacency[0, 0], 0, 1)
-    owner = links // TILES
-    places = slot_of(owner // N_GY, owner % N_GY) + links % TILES
+    links = jnp.transpose(adjacency, (0, 3, 1, 2)).reshape(NB, 1, TILES)
+    turned = jnp.swapaxes(block[0, 0], 0, 1)
     split, gram = pl.pallas_call(
         product_kernel,
         name="near_product",
@@ -243,29 +263,35 @@
             jax.ShapeDtypeStruct((2 * K, ROWS_DEV), jnp.bfloat16),
             jax.ShapeDtypeStruct((K, 2 * K), jnp.float32),
         ),
-        in_specs=[any_space, any_space, smem],
+        in_specs=[hbm, hbm, hbm],
         out_specs=(vmem, vmem),
         scratch_shapes=[
             pltpu.VMEM((TILES, NB, TILE, TILE), jnp.bfloat16),
             pltpu.VMEM((16 * TILES, K, TILE), jnp.bfloat16),
             pltpu.VMEM((K, ROWS_DEV), jnp.bfloat16),
+            pltpu.SMEM((NB, 1, TILES), jnp.int32),
             pltpu.VMEM((N_GX, K // 2, 2 * K), jnp.float32),
             pltpu.VMEM((N_GY, K // 2, 2 * K), jnp.float32),
             dma((A_COPIES,)),
             dma,
             dma((2, CHUNKS)),
             dma((2, CHUNKS)),
-            dma((2, 3, CHUNKS)),
-            dma((2, 3, CHUNKS)),
+            dma((3, CHUNKS)),
+            dma((3, CHUNKS)),
+            dma((3, CHUNKS)),
+            dma((3, CHUNKS)),
+            dma((2, TURNED)),
+            dma((2, TURNED)),
             dma((N_GX,)),
             dma((N_GX,)),
             dma((N_GY,)),
             dma((N_GY,)),
+            dma,
         ],
         compiler_params=pltpu.CompilerParams(
-            collective_id=0, has_side_effects=True, vmem_limit_bytes=56 * 1024 * 1024
+            collective_id=0, has_side_effects=True, vmem_limit_bytes=40 * 1024 * 1024
         ),
-    )(near_tiles[0, 0], jnp.swapaxes(block[0, 0], 0, 1), places)
+    )(near_tiles[0, 0], *(pltpu.with_memory_space_constraint(x, pltpu.HBM) for x in (turned, links)))
     basis, factor = pl.pallas_call(
         basis_kernel,
         name="orthonormal_basis",
@@ -273,13 +299,13 @@
             jax.ShapeDtypeStruct((K, ROWS_DEV), jnp.float32),
             jax.ShapeDtypeStruct((K, K), jnp.float32),
         ),
-        in_specs=[vmem, any_space],
-        out_specs=(any_space, vmem),
+        in_specs=[vmem, vmem],
+        out_specs=(hbm, vmem),
         scratch_shapes=[
-            pltpu.VMEM((2 * K, ROWS_DEV), jnp.bfloat16),
             pltpu.VMEM((K, ROWS_DEV), jnp.float32),
-            dma((BASIS_PARTS + 1,)),
+            dma((BASIS_PARTS,)),
         ],
+        compiler_params=pltpu.CompilerParams(vmem_limit_bytes=8 * 1024 * 1024),
     )(gram, split)
     return (jnp.swapaxes(basis, 0, 1).reshape(1, 1, ROWS_DEV, K), factor)
 

time: 54 us -> 47.1 us (0.87)
  Pallas kernels: 51.6 us -> 46.3 us
  other arithmetic: 1.34 us -> 0 us
    pallas_call x1, Pallas kernels: 46.3 us -> 42.7 us  [shards(): pl.pallas_call(product_kernel, name='near_product', out_shape=(jax.ShapeD...]
    pallas_call x1, Pallas kernels: 5.27 us -> 3.63 us  [shards(): pl.pallas_call(basis_kernel, name='orthonormal_basis', out_shape=(jax.Sha...]
    add x1 -> x0, other arithmetic: 1.34 us -> none  [shards(): places = slot_of(owner // N_GY, owner % N_GY) + links % TILES]
where the time goes in v2:
time: 47.1 us; the launch traced here: 46.9 us
  Pallas kernels  46.3 us (98%)
  between operations  0.64 us (1%)
    pallas_call x1, Pallas kernels, shards(): pl.pallas_call(product_kernel, name='near_product', out_shape=(jax.ShapeD...  42.7 us
    pallas_call x1, Pallas kernels, shards(): pl.pallas_call(basis_kernel, name='orthonormal_basis', out_shape=(jax.Sha...  3.63 us

profile of v2, /device:TPU:1, one launch (start us, length us, event | category | flops | bytes accessed | tf_op | source)
XLA Modules:
  0.0 46.9 jit_solution(8255568891840684830)
XLA Ops:
  0.6 42.7 %near_product.1 = (bf16[128,4096]{1,0:T(8,128)(2,1)S(1)}, f32[64,128]{1,0:T(8,128)S(1)}) custom-call(bf16[32,20,128,128]{3,2,1,0:T(8,128)(2,1)} %bitcast.10, bf16[64,4096]{1,0:T(8,128)(2,1)} %bitcast.11, s32[20,1,32]{2,1,0:T(1,128)} %bitcast.12), custom_call_target="tpu_custom_call" | custom-call | tf_op jit(solution)/shard_map/near_product/pallas_call | solution.py:259
  43.3 3.6 %orthonormal_basis.1 = (f32[64,4096]{1,0:T(8,128)}, f32[64,64]{1,0:T(8,128)}) custom-call(f32[64,128]{1,0:T(8,128)S(1)} %get-tuple-element.6.gram_ref, bf16[128,4096]{1,0:T(8,128)(2,1)S(1)} %get-tuple-element.7.split), custom_call_target="tpu_custom_call" | custom-call | tf_op jit(solution)/shard_map/orthonormal_basis/pallas_call | solution.py:295

commit v3 on v2

--- a/solution.py
+++ b/solution.py
@@ -20,7 +20,7 @@
 TURN_AT = 2
 PART = TILES // CHUNKS
 A_COPIES = 8
-UNROLL = 8
+UNROLL = TILES
 MESH = pl.DeviceIdType.MESH
 
 
@@ -54,6 +54,10 @@
     far_x = ring_x(2 * core - 1)
     own = slot_of(me_x, me_y)
 
+    own_copy = pltpu.make_async_copy(block_hbm, turned, own_sem)
+    own_copy.start()
+    links_copy = pltpu.make_async_copy(links_hbm, links, links_sem)
+    links_copy.start()
     barrier = pltpu.get_barrier_semaphore()
 
     def greet(x, y):
@@ -63,10 +67,6 @@
         greet(me_x, ring_y(step))
     for step in sorted(range(1, N_GX), key=lambda n: min(n, N_GX - n)):
         greet(ring_x(step), me_y)
-    own_copy = pltpu.make_async_copy(block_hbm, turned, own_sem)
-    own_copy.start()
-    links_copy = pltpu.make_async_copy(links_hbm, links, links_sem)
-    links_copy.start()
     own_copy.wait()
     for i in range(TILES):
         table[own + i] = turned[:, i * TILE : (i + 1) * TILE]
@@ -189,29 +189,29 @@
     def spread(x):
         return jnp.broadcast_to(x, (8, 128))
 
-    pivots = []
-    for p in range(count):
+    pivots = [zero] * count
+    for first in range(0, K, PANEL):
         columns = [
-            {r: spread(rows[r][:, 8 * p + j : 8 * p + j + 1]) for r in range(p, count)} for j in range(8)
+            {r: spread(rows[r][:, first + j : first + j + 1]) for r in range(first // 8, count)} for j in range(PANEL)
         ]
-        found = zero
-        for j in range(8):
-            pivot = spread(columns[j][p][j : j + 1])
-            found = jnp.where(sub == j, pivot, found)
+        for j in range(PANEL):
+            p, at = divmod(first + j, 8)
+            pivot = spread(columns[j][p][at : at + 1])
+            pivots[p] = jnp.where(sub == at, pivot, pivots[p])
             inverse = 1.0 / pivot
-            pivot_row = spread(rows[p][j : j + 1])
-            later = {i: spread(columns[i][p][j : j + 1]) for i in range(j + 1, 8)}
+            pivot_row = spread(rows[p][at : at + 1])
+            later = {i: spread(columns[i][p][at : at + 1]) for i in range(j + 1, PANEL)}
             for r in range(p, count):
                 scaled = columns[j][r] * inverse
                 if r == p:
-                    scaled = jnp.where(sub > j, scaled, zero)
-                for i in range(j + 1, 8):
+                    scaled = jnp.where(sub > at, scaled, zero)
+                for i in range(j + 1, PANEL):
                     columns[i][r] = columns[i][r] - scaled * later[i]
                 rows[r] = rows[r] - scaled * pivot_row
-        pivots.append(found)
     return rows, pivots
 
 
+PANEL = 16
 BASIS_PARTS = 4
 
 

time: 47.1 us -> 46.2 us (0.981)
  Pallas kernels: 46.3 us -> 45.5 us
    pallas_call x1, Pallas kernels: 42.7 us -> 42.1 us  [shards(): pl.pallas_call(product_kernel, name='near_product', out_shape=(jax.ShapeD...]
where the time goes in v3:
time: 46.2 us; the launch traced here: 46.1 us
  Pallas kernels  45.5 us (98%)
  between operations  0.64 us (1%)
    pallas_call x1, Pallas kernels, shards(): pl.pallas_call(product_kernel, name='near_product', out_shape=(jax.ShapeD...  42.1 us
    pallas_call x1, Pallas kernels, shards(): pl.pallas_call(basis_kernel, name='orthonormal_basis', out_shape=(jax.Sha...  3.37 us

profile of v3, /device:TPU:1, one launch (start us, length us, event | category | flops | bytes accessed | tf_op | source)
XLA Modules:
  0.0 46.1 jit_solution(14311878336616114095)
XLA Ops:
  0.6 42.1 %near_product.1 = (bf16[128,4096]{1,0:T(8,128)(2,1)S(1)}, f32[64,128]{1,0:T(8,128)S(1)}) custom-call(bf16[32,20,128,128]{3,2,1,0:T(8,128)(2,1)} %bitcast.10, bf16[64,4096]{1,0:T(8,128)(2,1)} %bitcast.11, s32[20,1,32]{2,1,0:T(1,128)} %bitcast.12), custom_call_target="tpu_custom_call" | custom-call | tf_op jit(solution)/shard_map/near_product/pallas_call | solution.py:259
  42.7 3.4 %orthonormal_basis.1 = (f32[64,4096]{1,0:T(8,128)}, f32[64,64]{1,0:T(8,128)}) custom-call(f32[64,128]{1,0:T(8,128)S(1)} %get-tuple-element.6.gram_ref, bf16[128,4096]{1,0:T(8,128)(2,1)S(1)} %get-tuple-element.7.split), custom_call_target="tpu_custom_call" | custom-call | tf_op jit(solution)/shard_map/orthonormal_basis/pallas_call | solution.py:295

commit v4 on v3

--- a/solution.py
+++ b/solution.py
@@ -21,6 +21,7 @@
 PART = TILES // CHUNKS
 A_COPIES = 8
 UNROLL = TILES
+FOLDED = 24
 MESH = pl.DeviceIdType.MESH
 
 
@@ -31,8 +32,29 @@
 def folded(gram):
     rows = gram[:K] + gram[K:]
     both = rows + pltpu.roll(rows, K, 1)
-    lane = lax.broadcasted_iota(jnp.int32, (K // 2, 2 * K), 1)
-    return jnp.where(lane < K, both[: K // 2], both[K // 2 :])
+    lane = lax.broadcasted_iota(jnp.int32, (16, 2 * K), 1)
+    top = jnp.where(lane < K, both[:16], both[16:32])
+    lane = lane[:8]
+    low = both[32:]
+    moved = pltpu.roll(low, 32, 1)
+    corner = jnp.where(
+        lane < 64,
+        jnp.where(lane < 32, moved[:8], low[8:16]),
+        jnp.where(lane < 96, moved[16:24], low[24:]),
+    )
+    return jnp.concatenate([top, corner], axis=0)
+
+
+def unfolded(packed):
+    top, corner = packed[:16], packed[16:]
+    upper = jnp.concatenate([top, pltpu.roll(top, K, 1)], axis=0)
+    square = jnp.concatenate([upper, jnp.zeros((96, 2 * K), jnp.float32)], axis=0)
+    left = square.T[32:64]
+    right = jnp.concatenate(
+        [pltpu.roll(corner, 32, 1), corner, pltpu.roll(corner, 96, 1), pltpu.roll(corner, 64, 1)], axis=0
+    )
+    lane = lax.broadcasted_iota(jnp.int32, (32, 2 * K), 1)
+    return jnp.concatenate([upper, jnp.where(lane < 32, left, right)], axis=0)
 
 
 def product_kernel(
@@ -149,7 +171,7 @@
     image = split[...]
     gram = lax.dot_general(image, image, (((1,), (1,)), ((), ())), preferred_element_type=jnp.float32)
 
-    def summed(value, gathered, count, me, send, recv, device):
+    def summed(value, gathered, count, me, send, recv, device, earlier):
         gathered[me] = value
         sends = []
         for step in range(1, count):
@@ -159,6 +181,8 @@
             )
             copy.start()
             sends.append(copy)
+        for copy in earlier:
+            copy.wait_send()
         for step in range(1, count):
             source = gathered.at[lax.rem(me - step + count, count)]
             pltpu.make_async_copy(source, source, recv.at[step]).wait()
@@ -168,16 +192,13 @@
         return terms[0], sends
 
     partial, sends_x = summed(
-        folded(gram), across_x, N_GX, me_x, sx_send, sx_recv, lambda step: (ring_x(step), me_y)
+        folded(gram), across_x, N_GX, me_x, sx_send, sx_recv, lambda step: (ring_x(step), me_y), started
     )
     total, sends_y = summed(
-        partial, across_y, N_GY, me_y, sy_send, sy_recv, lambda step: (me_x, ring_y(step))
-    )
-    swapped = pltpu.roll(total, K, 1)
-    lane = lax.broadcasted_iota(jnp.int32, total.shape, 1)
-    gram_ref[: K // 2] = jnp.where(lane < K, total, swapped)
-    gram_ref[K // 2 :] = jnp.where(lane < K, swapped, total)
-    for copy in started + sends_x + sends_y:
+        partial, across_y, N_GY, me_y, sy_send, sy_recv, lambda step: (me_x, ring_y(step)), sends_x
+    )
+    gram_ref[...] = unfolded(total)
+    for copy in sends_y:
         copy.wait_send()
 
 
@@ -212,7 +233,7 @@
 
 
 PANEL = 16
-BASIS_PARTS = 4
+BASIS_PARTS = 8
 
 
 def basis_kernel(gram_ref, split, basis_hbm, factor_ref, basis, sems):
@@ -236,13 +257,13 @@
         high = solve.astype(jnp.bfloat16)
         highs.append(high)
         lows.append((solve - high.astype(jnp.float32)).astype(jnp.bfloat16))
-    solver = jnp.concatenate([jnp.concatenate(highs, 0), jnp.concatenate(lows, 0)], 1)
+    solver = jnp.concatenate(highs + lows, 0)
     width = ROWS_DEV // BASIS_PARTS
     stores = []
     for part in range(BASIS_PARTS):
         here = slice(part * width, (part + 1) * width)
-        image = split[:, here]
-        basis[:, here] = jnp.dot(solver, jnp.concatenate([image, image], 0), preferred_element_type=jnp.float32)
+        products = jnp.dot(solver, split[:, here], preferred_element_type=jnp.float32)
+        basis[:, here] = products[:K] + products[K:]
         at = pl.ds(part * width, width)
         store = pltpu.make_async_copy(basis.at[:, at], basis_hbm.at[:, at], sems.at[part])
         store.start()
@@ -270,8 +291,8 @@
             pltpu.VMEM((16 * TILES, K, TILE), jnp.bfloat16),
             pltpu.VMEM((K, ROWS_DEV), jnp.bfloat16),
             pltpu.SMEM((NB, 1, TILES), jnp.int32),
-            pltpu.VMEM((N_GX, K // 2, 2 * K), jnp.float32),
-            pltpu.VMEM((N_GY, K // 2, 2 * K), jnp.float32),
+            pltpu.VMEM((N_GX, FOLDED, 2 * K), jnp.float32),
+            pltpu.VMEM((N_GY, FOLDED, 2 * K), jnp.float32),
             dma((A_COPIES,)),
             dma,
             dma((2, CHUNKS)),

time: 46.2 us -> 45.6 us (0.987)
  Pallas kernels: 45.5 us -> 44.9 us
    pallas_call x1, Pallas kernels: 42.1 us -> 41.5 us  [shards(): pl.pallas_call(product_kernel, name='near_product', out_shape=(jax.ShapeD...]
where the time goes in v4:
time: 45.6 us; the launch traced here: 45.5 us
  Pallas kernels  44.9 us (98%)
  between operations  0.64 us (1%)
    pallas_call x1, Pallas kernels, shards(): pl.pallas_call(product_kernel, name='near_product', out_shape=(jax.ShapeD...  41.5 us
    pallas_call x1, Pallas kernels, shards(): pl.pallas_call(basis_kernel, name='orthonormal_basis', out_shape=(jax.Sha...  3.37 us

profile of v4, /device:TPU:1, one launch (start us, length us, event | category | flops | bytes accessed | tf_op | source)
XLA Modules:
  0.0 45.5 jit_solution(10835790495432404505)
XLA Ops:
  0.6 41.5 %near_product.1 = (bf16[128,4096]{1,0:T(8,128)(2,1)S(1)}, f32[64,128]{1,0:T(8,128)S(1)}) custom-call(bf16[32,20,128,128]{3,2,1,0:T(8,128)(2,1)} %bitcast.10, bf16[64,4096]{1,0:T(8,128)(2,1)} %bitcast.11, s32[20,1,32]{2,1,0:T(1,128)} %bitcast.12), custom_call_target="tpu_custom_call" | custom-call | tf_op jit(solution)/shard_map/near_product/pallas_call | solution.py:280
  42.1 3.4 %orthonormal_basis.1 = (f32[64,4096]{1,0:T(8,128)}, f32[64,64]{1,0:T(8,128)}) custom-call(f32[64,128]{1,0:T(8,128)S(1)} %get-tuple-element.6.gram_ref, bf16[128,4096]{1,0:T(8,128)(2,1)S(1)} %get-tuple-element.7.split), custom_call_target="tpu_custom_call" | custom-call | tf_op jit(solution)/shard_map/orthonormal_basis/pallas_call | solution.py:316

commit v5 on v4

--- a/solution.py
+++ b/solution.py
@@ -17,7 +17,7 @@
 ROWS = ROWS_DEV * N_GX * N_GY
 CHUNKS = 4
 TURNED = 1
-TURN_AT = 2
+TURN_AT = 1
 PART = TILES // CHUNKS
 A_COPIES = 8
 UNROLL = TILES

time: 45.6 us -> 45.6 us (level)
  no operation moved by 1% of the time
where the time goes in v5:
time: 45.6 us; the launch traced here: 45.5 us
  Pallas kernels  44.9 us (98%)
  between operations  0.64 us (1%)
    pallas_call x1, Pallas kernels, shards(): pl.pallas_call(product_kernel, name='near_product', out_shape=(jax.ShapeD...  41.5 us
    pallas_call x1, Pallas kernels, shards(): pl.pallas_call(basis_kernel, name='orthonormal_basis', out_shape=(jax.Sha...  3.37 us

profile of v5, /device:TPU:1, one launch (start us, length us, event | category | flops | bytes accessed | tf_op | source)
XLA Modules:
  0.0 45.5 jit_solution(12602354278135965524)
XLA Ops:
  0.6 41.5 %near_product.1 = (bf16[128,4096]{1,0:T(8,128)(2,1)S(1)}, f32[64,128]{1,0:T(8,128)S(1)}) custom-call(bf16[32,20,128,128]{3,2,1,0:T(8,128)(2,1)} %bitcast.10, bf16[64,4096]{1,0:T(8,128)(2,1)} %bitcast.11, s32[20,1,32]{2,1,0:T(1,128)} %bitcast.12), custom_call_target="tpu_custom_call" | custom-call | tf_op jit(solution)/shard_map/near_product/pallas_call | solution.py:280
  42.1 3.4 %orthonormal_basis.1 = (f32[64,4096]{1,0:T(8,128)}, f32[64,64]{1,0:T(8,128)}) custom-call(f32[64,128]{1,0:T(8,128)S(1)} %get-tuple-element.6.gram_ref, bf16[128,4096]{1,0:T(8,128)(2,1)S(1)} %get-tuple-element.7.split), custom_call_target="tpu_custom_call" | custom-call | tf_op jit(solution)/shard_map/orthonormal_basis/pallas_call | solution.py:316
